TPU v7x, 32 devices: a whole 2x2x4 slice. The times are simulated.
32 devices in a mesh: gx: 4 (over y, x), gy: 8 (over z, core).
Axes of the slice: x: 2, y: 2, z: 4, core: 2. Of those that a mesh axis runs over, the one named last changes fastest.
Arguments:
- vertex_state: bfloat16 [256, 256, 128], P(('gx', 'gy')), may hold values from -6 to 6
- edge_state: bfloat16 [256, 1536, 128], P(('gx', 'gy')), may hold values from -6 to 6
- senders: int32 [256, 1536], P(('gx', 'gy')), may hold values from 0 to 511
- receivers: int32 [256, 1536], P(('gx', 'gy')), may hold values from 0 to 255
- counts: int32 [256], P(('gx', 'gy')), may hold values from 768 to 1536
- border_rows: int32 [256, 2, 128], P(('gx', 'gy')), may hold values from 0 to 255
- old_neighbours: int32 [256, 2], P(('gx', 'gy')), may hold values from 0 to 255, as said below
- new_neighbours: int32 [256, 2], P(('gx', 'gy')), may hold values from 0 to 255, as said below
- new_place: int32 [256], P(('gx', 'gy')), may hold values from 0 to 255, as said below
- weights_in: bfloat16 [3, 5, 128, 128], replicated, may hold values from -0.5 to 0.5
- weights_out: bfloat16 [3, 2, 128, 128], replicated, may hold values from -0.5 to 0.5
- biases: float32 [3, 6, 128], replicated, may hold values from -3 to 3
- norm_gains: float32 [3, 2, 128], replicated, may hold values from 0.25 to 1.75
Outputs:
- vertex_out: bfloat16 [256, 256, 128], P(('gx', 'gy'))
- edge_out: bfloat16 [256, 1536, 128], P(('gx', 'gy'))
Inputs may be any that keep to these rules, and one draw needn't show every extreme that they name: A permutation of the patches. With devices numbered gx-index times the size of gy plus gy-index, patch p stands on device p // 8 and moves to device new_place[p] // 8, which has the same gx-index; one device sends at most 1 patch to any one device, and some pair of devices reaches 1. old_neighbours[p, 0] stands on the device whose gy-index is one less than that of p's device (cyclically) and whose gx-index is the same; old_neighbours[p, 1] on the device whose gx-index is one less (cyclically) and whose gy-index is the same. new_neighbours[new_place[p], k] = new_place[old_neighbours[p, k]]; in the new positions it follows the same rule as old_neighbours.
All inputs are finite; a program needn't handle non-finite values.
Results may differ from a plain program's by a relative error of at most 0.0066.
Values may be sent and summed in bfloat16 or wider, within the bound.
A program may use at most 128 MiB of HBM per device.

v0:
```python
import jax
import jax.numpy as jnp
from jax import lax
from jax.sharding import PartitionSpec as P

STEPS_OLD = 2


def shifted(shard, axis, by):
    devices = lax.axis_size(axis)
    return lax.ppermute(shard, axis, [(i, (i + by) % devices) for i in range(devices)])


def product(left, right):
    return jnp.dot(left, right, preferred_element_type=jnp.float32)


def normalize(values, scale_row, shift_row):
    center = values - jnp.mean(values, axis=-1, keepdims=True)
    spread = jnp.mean(center * center, axis=-1, keepdims=True)
    return center * lax.rsqrt(spread + 1e-05) * scale_row + shift_row


def picker(indices, offset, number):
    columns = offset + jnp.arange(number, dtype=jnp.int32)
    return (indices[:, None] == columns[None, :]).astype(jnp.bfloat16)


def fetch_ghosts(vertex_state, border_rows, neighbour_slots):
    patch_rows = jnp.arange(vertex_state.shape[0], dtype=jnp.int32)[:, None]
    along_gy = vertex_state[patch_rows, border_rows[:, 0]]
    along_gx = vertex_state[patch_rows, border_rows[:, 1]]
    came_gy = shifted(along_gy, "gy", 1)
    came_gx = shifted(along_gx, "gx", 1)
    return jnp.concatenate([came_gy[neighbour_slots[:, 0]], came_gx[neighbour_slots[:, 1]]], axis=1)


def edge_start(layer_weights, pieces):
    weights_in, weights_out, bias_rows, gain_rows = layer_weights
    vertex_block, edge_block, sender_ids, receiver_ids = pieces
    vertex_count = vertex_block.shape[0]
    receiver_terms = product(vertex_block, weights_in[2]).astype(jnp.bfloat16)
    started = product(edge_block, weights_in[0]) + product(
        picker(receiver_ids, 0, vertex_count), receiver_terms
    )
    started = started + bias_rows[0]
    own_terms = product(vertex_block, weights_in[1]).astype(jnp.bfloat16)
    started = started + product(picker(sender_ids, 0, vertex_count), own_terms)
    return started


def patch_finish(layer_weights, pieces):
    weights_in, weights_out, bias_rows, gain_rows = layer_weights
    vertex_block, ghost_block, edge_block, sender_ids, receiver_ids, edge_count, started = pieces
    vertex_count = vertex_block.shape[0]
    ghost_count = ghost_block.shape[0]
    edge_total = edge_block.shape[0]
    ghost_terms = product(ghost_block, weights_in[1]).astype(jnp.bfloat16)
    summed = started + product(picker(sender_ids, vertex_count, ghost_count), ghost_terms)
    edge_hidden = jax.nn.relu(summed).astype(jnp.bfloat16)
    edge_update = normalize(
        product(edge_hidden, weights_out[0]) + bias_rows[1], gain_rows[0], bias_rows[2]
    )
    live = jnp.arange(edge_total, dtype=jnp.int32) < edge_count
    widened = edge_block.astype(jnp.float32)
    fresh_edges = jnp.where(live[:, None], widened + edge_update, widened).astype(jnp.bfloat16)
    vertex_ids = jnp.arange(vertex_count, dtype=jnp.int32)
    incoming = ((vertex_ids[:, None] == receiver_ids[None, :]) & live[None, :]).astype(jnp.bfloat16)
    aggregate = product(incoming, fresh_edges).astype(jnp.bfloat16)
    node_hidden = (
        product(vertex_block, weights_in[3]) + product(aggregate, weights_in[4]) + bias_rows[3]
    )
    node_hidden = jax.nn.relu(node_hidden).astype(jnp.bfloat16)
    vertex_update = normalize(
        product(node_hidden, weights_out[1]) + bias_rows[4], gain_rows[1], bias_rows[5]
    )
    fresh_vertices = (vertex_block.astype(jnp.float32) + vertex_update).astype(jnp.bfloat16)
    return (fresh_vertices, fresh_edges)


def run_step(layer_weights, vertex_state, edge_state, senders, receivers, counts, ghosts):
    started = lax.map(
        lambda pieces: edge_start(layer_weights, pieces),
        (vertex_state, edge_state, senders, receivers),
    )
    return lax.map(
        lambda pieces: patch_finish(layer_weights, pieces),
        (vertex_state, ghosts, edge_state, senders, receivers, counts, started),
    )


def local(
    vertex_state,
    edge_state,
    senders,
    receivers,
    counts,
    border_rows,
    old_neighbours,
    new_neighbours,
    new_place,
    weights_in,
    weights_out,
    biases,
    norm_gains,
):
    patch_count = vertex_state.shape[0]
    edge_total = edge_state.shape[1]

    def weights_of(step_index):
        return (
            weights_in[step_index],
            weights_out[step_index],
            biases[step_index],
            norm_gains[step_index],
        )

    neighbour_slots = old_neighbours % patch_count
    for step_index in range(STEPS_OLD):
        ghosts = fetch_ghosts(vertex_state, border_rows, neighbour_slots)
        vertex_state, edge_state = run_step(
            weights_of(step_index), vertex_state, edge_state, senders, receivers, counts, ghosts
        )
    cycle_size = lax.axis_size("gy")
    capacity = (patch_count + cycle_size - 1) // cycle_size
    target = new_place // patch_count
    target_gy = target % cycle_size
    target_slot = new_place % patch_count
    positions = jnp.arange(patch_count, dtype=jnp.int32)
    earlier = (target_gy[:, None] == target_gy[None, :]) & (positions[:, None] > positions[None, :])
    before = jnp.sum(earlier.astype(jnp.int32), axis=1)
    place_index = target_gy * capacity + before
    outbox = cycle_size * capacity
    outbox_ids = jnp.arange(outbox, dtype=jnp.int32)
    filled = place_index[None, :] == outbox_ids[:, None]
    source = jnp.sum(jnp.where(filled, positions[None, :], 0), axis=1)
    occupied = jnp.any(filled, axis=1)
    id_rows = jnp.concatenate([senders, receivers, border_rows.reshape(patch_count, -1)], axis=1)[
        source
    ]
    header = jnp.stack([jnp.where(occupied, target_slot[source], -1), counts[source]], axis=1)
    arrived = (
        lax.all_to_all(vertex_state[source], "gy", split_axis=0, concat_axis=0, tiled=True),
        lax.all_to_all(edge_state[source], "gy", split_axis=0, concat_axis=0, tiled=True),
        lax.all_to_all(id_rows, "gy", split_axis=0, concat_axis=0, tiled=True),
        lax.all_to_all(header, "gy", split_axis=0, concat_axis=0, tiled=True),
    )
    landing = arrived[3][:, 0]
    chosen = jnp.sum(
        jnp.where(landing[None, :] == positions[:, None], outbox_ids[None, :], 0), axis=1
    )
    vertex_state = arrived[0][chosen]
    edge_state = arrived[1][chosen]
    id_rows = arrived[2][chosen]
    counts = arrived[3][chosen, 1]
    senders = id_rows[:, :edge_total]
    receivers = id_rows[:, edge_total : 2 * edge_total]
    border_rows = id_rows[:, 2 * edge_total :].reshape(patch_count, 2, -1)
    neighbour_slots = new_neighbours % patch_count
    step_index = 0
    ghosts = fetch_ghosts(vertex_state, border_rows, neighbour_slots)
    vertex_state, edge_state = run_step(
        weights_of(STEPS_OLD + step_index),
        vertex_state,
        edge_state,
        senders,
        receivers,
        counts,
        ghosts,
    )
    return (vertex_state, edge_state)


def solution(mesh):
    placed = (
        P(("gx", "gy"), None, None),
        P(("gx", "gy"), None, None),
        P(("gx", "gy"), None),
        P(("gx", "gy"), None),
        P(("gx", "gy")),
        P(("gx", "gy"), None, None),
        P(("gx", "gy"), None),
        P(("gx", "gy"), None),
        P(("gx", "gy")),
        P(),
        P(),
        P(),
        P(),
    )
    return jax.shard_map(
        local,
        mesh=mesh,
        in_specs=placed,
        out_specs=(P(("gx", "gy"), None, None), P(("gx", "gy"), None, None)),
        check_vma=False,
    )
```

profile of v0, /device:TPU:0, one launch (start us, length us, event | category | flops | bytes accessed | tf_op | source)
XLA Modules:
  0.0 464.2 jit_solution(15381699110809271963)
XLA Ops:
  1.5 17.9 %gather_fusion = bf16[1024,128]{1,0:T(8,128)(2,1)} fusion(bf16[8,256,128]{2,1,0:T(8,128)(2,1)} %param.25, s32[1024]{0:T(1024)S(1)} %fusion.237), kind=kCustom, calls=%fused_computation | custom fusion | bytes 532480 | tf_op jit(solution)/shard_map/gather | solution.py:31
  19.9 10.5 %gather_fusion.2 = bf16[1024,128]{1,0:T(8,128)(2,1)} fusion(bf16[8,256,128]{2,1,0:T(8,128)(2,1)S(1)} %copy-done.1, s32[1024]{0:T(1024)S(1)} %fusion.241), kind=kCustom, calls=%fused_computation.2 | custom fusion | bytes 532480 | tf_op jit(solution)/shard_map/gather | solution.py:32
  30.5 2.5 collective-permute-start.1
  35.4 4.9 %all-to-all-start.1 = ((s32[8,1,2]{2,1,0:T(1,128)}), s32[8,1,2]{2,1,0:T(1,128)S(1)}, u32[]{:S(2)}, u32[]{:S(2)}) async-start(s32[8,1,2]{2,1,0:T(1,128)} %copy.72), calls=%async_computation.1 | async-start | bytes 8192 | tf_op jit(solution)/shard_map/all_to_all | solution.py:146
  40.4 3.2 broadcast.346.clone
  43.6 26.2 %while.66 = (s32[]{:T(128)}, f32[8,1536,128]{2,1,0:T(8,128)}, bf16[8,1536,128]{2,1,0:T(8,128)(2,1)}, bf16[5,128,128]{2,1,0:T(8,128)(2,1)S(1)}, s32[8,1536]{1,0:T...) while((s32[]{:T(128)}, f32[8,1536,128]{2,1,0:T(8,128)}, ...), condition=%wide.region_1.2_spmd, body=%wide.region_0.1_spmd.sunk | while | flops 269877248 | bytes 4598885 | solution.py:82
  76.1 2.0 broadcast.345.clone.1
  78.1 62.8 %while.67 = (s32[]{:T(128)}, bf16[8,256,128]{1,2,0:T(8,128)(2,1)S(1)}, bf16[8,1536,128]{1,2,0:T(8,128)(2,1)}, bf16[8,256,128]{2,1,0:T(8,128)(2,1)S(1)}, bf16[5,1...) while((s32[]{:T(128)}, ...), condition=%wide.region_7.8_spmd, body=%wide.region_2.7_spmd.sunk | while | flops 290131456 | bytes 8022189 | solution.py:86
  79.1 1.8 fusion.379
  87.0 1.8 fusion.379
  94.8 1.8 fusion.379
  102.7 1.8 fusion.379
  110.5 1.8 fusion.379
  141.2 10.5 %gather_fusion.4 = bf16[1024,128]{1,0:T(8,128)(2,1)} fusion(bf16[8,256,128]{2,1,0:T(8,128)(2,1)S(1)} %copy.68, s32[1024]{0:T(1024)S(1)} %fusion.237), kind=kCustom, calls=%fused_computation.4 | custom fusion | bytes 532480 | tf_op jit(solution)/shard_map/gather | solution.py:31
  151.7 10.5 %gather_fusion.6 = bf16[1024,128]{1,0:T(8,128)(2,1)} fusion(bf16[8,256,128]{2,1,0:T(8,128)(2,1)S(1)} %copy.68, s32[1024]{0:T(1024)S(1)} %fusion.241), kind=kCustom, calls=%fused_computation.6 | custom fusion | bytes 532480 | tf_op jit(solution)/shard_map/gather | solution.py:32
  164.3 3.2 broadcast.346.clone.1
  167.4 26.6 %while.68 = (s32[]{:T(128)}, f32[8,1536,128]{2,1,0:T(8,128)}, bf16[8,1536,128]{1,2,0:T(8,128)(2,1)}, bf16[5,128,128]{2,1,0:T(8,128)(2,1)S(1)}, s32[8,1536]{1,0:T...) while((s32[]{:T(128)}, f32[8,1536,128]{2,1,0:T(8,128)}, ...), condition=%wide.region_9.10_spmd, body=%wide.region_8.9_spmd.sunk | while | flops 269877248 | bytes 4598885 | solution.py:82
  198.0 4.7 %all-to-all-start.2 = ((s32[8,1,3328]{2,1,0:T(1,128)}), s32[8,1,3328]{2,1,0:T(1,128)S(1)}, u32[]{:S(2)}, u32[]{:S(2)}) async-start(s32[8,1,3328]{2,1,0:T(1,128)} %copy.74), calls=%async_computation.2 | async-start | bytes 212992 | tf_op jit(solution)/shard_map/all_to_all | solution.py:145
  202.7 1.9 broadcast.345
  204.7 61.6 %while.69 = (s32[]{:T(128)}, bf16[8,256,128]{2,1,0:T(8,128)(2,1)S(1)}, bf16[8,1536,128]{1,2,0:T(8,128)(2,1)}, bf16[8,256,128]{1,2,0:T(8,128)(2,1)S(1)}, bf16[5,1...) while((s32[]{:T(128)}, ...), condition=%wide.region_15.16_spmd, body=%wide.region_10.15_spmd.sunk | while | flops 290131456 | bytes 6449325 | solution.py:86
  209.0 2.1 bitcast_dynamic-update-slice_fusion.5
  216.7 2.1 bitcast_dynamic-update-slice_fusion.5
  224.4 2.1 bitcast_dynamic-update-slice_fusion.5
  232.1 2.1 bitcast_dynamic-update-slice_fusion.5
  239.8 2.1 bitcast_dynamic-update-slice_fusion.5
  247.5 2.1 bitcast_dynamic-update-slice_fusion.5
  255.2 2.1 bitcast_dynamic-update-slice_fusion.5
  262.9 2.1 bitcast_dynamic-update-slice_fusion.5
  267.7 5.1 %all-to-all-start = ((bf16[8,256,128]{2,1,0:T(8,128)(2,1)}), bf16[8,256,128]{2,1,0:T(8,128)(2,1)S(1)}, u32[]{:S(2)}, u32[]{:S(2)}) async-start(bf16[8,256,128]{2,1,0:T(8,128)(2,1)} %gather_fusion.8), calls=%async_computation | async-start | bytes 1048576 | tf_op jit(solution)/shard_map/all_to_all | solution.py:143
  272.8 4.3 gather_fusion.15
  277.1 11.0 %all-to-all-done = bf16[8,256,128]{2,1,0:T(8,128)(2,1)S(1)} async-done(((bf16[8,256,128]{2,1,0:T(8,128)(2,1)}), bf16[8,256,128]{2,1,0:T(8,128)(2,1)S(1)}, u32[]{:S(2)}, u32[]{:S(2)}) %all-to-all-start) | async-done | bytes 524320 | tf_op jit(solution)/shard_map/all_to_all | solution.py:143
  288.1 4.4 all-to-all-start.3
  294.8 5.8 %gather_fusion.17 = bf16[1024,128]{1,0:T(8,128)(2,1)S(1)} fusion(bf16[8,256,128]{2,1,0:T(8,128)(2,1)S(1)} %gather_fusion.11, s32[1024]{0:T(1024)S(1)} %get-tuple-element.784), kind=kCustom, calls=%fused_computation.17 | custom fusion | bytes 532480 | tf_op jit(solution)/shard_map/gather | solution.py:31
  301.0 5.8 %gather_fusion.19 = bf16[1024,128]{1,0:T(8,128)(2,1)S(1)} fusion(bf16[8,256,128]{2,1,0:T(8,128)(2,1)S(1)} %gather_fusion.11, s32[1024]{0:T(1024)S(1)} %get-tuple-element.785), kind=kCustom, calls=%fused_computation.19 | custom fusion | bytes 532480 | tf_op jit(solution)/shard_map/gather | solution.py:32
  308.4 42.6 %collective-permute-done.4 = bf16[8,128,128]{2,1,0:T(8,128)(2,1)S(1)} collective-permute-done((bf16[8,128,128]{2,1,0:T(8,128)(2,1)S(1)}, bf16[8,128,128]{2,1,0:T(8,128)(2,1)S(1)}, u32[]{:S(2)}, u32[]{:S(2)}) %collective-permute-start.4) | collective-permute-done | bytes 262176 | tf_op jit(solution)/shard_map/ppermute | solution.py:11
  352.2 14.6 %all-to-all-done.3 = bf16[8,1536,128]{1,2,0:T(8,128)(2,1)} async-done(((bf16[8,1536,128]{1,2,0:T(8,128)(2,1)}), bf16[8,1536,128]{1,2,0:T(8,128)(2,1)}, u32[]{:S(2)}, u32[]{:S(2)}) %all-to-all-start.3) | async-done | bytes 3145760 | tf_op jit(solution)/shard_map/all_to_all | solution.py:144
  366.9 4.3 gather_fusion.16
  371.2 3.2 broadcast.346
  374.4 26.6 %while.70 = (s32[]{:T(128)}, f32[8,1536,128]{2,1,0:T(8,128)}, bf16[8,1536,128]{1,2,0:T(8,128)(2,1)}, bf16[5,128,128]{2,1,0:T(8,128)(2,1)S(1)}, s32[8,1536]{1,0:T...) while((s32[]{:T(128)}, f32[8,1536,128]{2,1,0:T(8,128)}, ...), condition=%wide.region_21.22_spmd, body=%wide.region_20.21_spmd.sunk | while | flops 269877248 | bytes 4598885 | solution.py:82
  401.8 62.4 %while.71 = (s32[]{:T(128)}, bf16[8,256,128]{2,1,0:T(8,128)(2,1)}, bf16[8,1536,128]{2,1,0:T(8,128)(2,1)}, bf16[8,256,128]{2,1,0:T(8,128)(2,1)S(1)}, bf16[5,128,1...) while((s32[]{:T(128)}, bf16[8,256,128]{2,1,0:T(8,128)(2,1)}, ...), condition=%wide.region_27.28_spmd, body=%wide.region_22.27_spmd.sunk | while | flops 290131456 | bytes 7891117 | solution.py:86
  402.0 1.8 fusion.427
  409.8 1.8 fusion.427
  417.6 1.8 fusion.427
  425.4 1.8 fusion.427
  433.2 1.8 fusion.427
  441.0 1.8 fusion.427
  448.8 1.8 fusion.427
  456.6 1.8 fusion.427
  (717 shorter events, 246.0 us)
Async XLA Ops:
  0.6 19.3 %copy-start.1 = (bf16[8,256,128]{2,1,0:T(8,128)(2,1)S(1)}, bf16[8,256,128]{2,1,0:T(8,128)(2,1)}, u32[]{:S(2)}) copy-start(bf16[8,256,128]{2,1,0:T(8,128)(2,1)} %param.25) | copy-start | bytes 1572868
  0.6 32.3 %copy-start.10 = (s32[8]{0:T(128)S(1)}, s32[8]{0:T(128)}, u32[]{:S(2)}) copy-start(s32[8]{0:T(128)} %param.33) | copy-start | bytes 100
  1.5 32.6 %copy-start = (s32[8]{0:T(128)S(1)}, s32[8]{0:T(128)}, u32[]{:S(2)}) copy-start(s32[8]{0:T(128)} %param.29) | copy-start | bytes 100
  1.5 38.8 %copy-start.8 = (s32[8,2]{0,1:T(2,128)S(1)}, s32[8,2]{0,1:T(2,128)}, u32[]{:S(2)}) copy-start(s32[8,2]{0,1:T(2,128)} %param.31) | copy-start | bytes 196
  1.5 38.9 %copy-start.4 = (bf16[3,5,128,128]{3,2,1,0:T(8,128)(2,1)S(1)}, bf16[3,5,128,128]{3,2,1,0:T(8,128)(2,1)}, u32[]{:S(2)}) copy-start(bf16[3,5,128,128]{3,2,1,0:T(8,128)(2,1)} %param.34) | copy-start | bytes 1474564
  19.4 21.0 %copy-start.6 = (f32[3,6,128]{2,1,0:T(8,128)S(1)}, f32[3,6,128]{2,1,0:T(8,128)}, u32[]{:S(2)}) copy-start(f32[3,6,128]{2,1,0:T(8,128)} %param.36) | copy-start | bytes 27652
  19.4 52.7 %collective-permute-start = (bf16[8,128,128]{2,1,0:T(8,128)(2,1)}, bf16[8,128,128]{2,1,0:T(8,128)(2,1)}, u32[]{:S(2)}, u32[]{:S(2)}) collective-permute-start(bf16[8,128,128]{2,1,0:T(8,128)(2,1)} %bitcast.82), channel_id=1, source_target_pairs={{0,1},{1,2},{2,3},{3,4},{4,5},{5,6},{6,7},{7,0},{8,9},{9,10},{10,1... | collective-permute-start | bytes 786440 | tf_op jit(solution)/shard_map/ppermute | solution.py:11
  30.5 43.2 %collective-permute-start.1 = (bf16[8,128,128]{2,1,0:T(8,128)(2,1)}, bf16[8,128,128]{2,1,0:T(8,128)(2,1)}, u32[]{:S(2)}, u32[]{:S(2)}) collective-permute-start(bf16[8,128,128]{2,1,0:T(8,128)(2,1)} %bitcast.86), channel_id=1, source_target_pairs={{0,8},{8,16},{16,24},{24,0},{1,9},{9,17},{17,25},{25,1},{2,10},{10... | collective-permute-start | bytes 786440 | tf_op jit(solution)/shard_map/ppermute | solution.py:11
  35.4 162.6 %all-to-all-start.1 = ((s32[8,1,2]{2,1,0:T(1,128)}), s32[8,1,2]{2,1,0:T(1,128)S(1)}, u32[]{:S(2)}, u32[]{:S(2)}) async-start(s32[8,1,2]{2,1,0:T(1,128)} %copy.72), calls=%async_computation.1 | async-start | bytes 8192 | tf_op jit(solution)/shard_map/all_to_all | solution.py:146
  40.4 3.2 copy-start.2
  40.4 3.2 copy-start.3
  43.6 26.2 %copy-start.7 = (f32[3,2,128]{2,1,0:T(2,128)S(1)}, f32[3,2,128]{2,1,0:T(2,128)}, u32[]{:S(2)}) copy-start(f32[3,2,128]{2,1,0:T(2,128)} %param.37) | copy-start | bytes 9220
  43.6 26.2 %copy-start.5 = (s32[8,2,128]{2,1,0:T(2,128)S(1)}, s32[8,2,128]{2,1,0:T(2,128)}, u32[]{:S(2)}) copy-start(s32[8,2,128]{2,1,0:T(2,128)} %param.30) | copy-start | bytes 24580
  162.3 31.8 %collective-permute-start.2 = (bf16[8,128,128]{2,1,0:T(8,128)(2,1)}, bf16[8,128,128]{2,1,0:T(8,128)(2,1)}, u32[]{:S(2)}, u32[]{:S(2)}) collective-permute-start(bf16[8,128,128]{2,1,0:T(8,128)(2,1)} %bitcast.92), channel_id=1, source_target_pairs={{0,1},{1,2},{2,3},{3,4},{4,5},{5,6},{6,7},{7,0},{8,9},{9,10},{10,1... | collective-permute-start | bytes 786440 | tf_op jit(solution)/shard_map/ppermute | solution.py:11
  162.8 32.8 %collective-permute-start.3 = (bf16[8,128,128]{2,1,0:T(8,128)(2,1)}, bf16[8,128,128]{2,1,0:T(8,128)(2,1)}, u32[]{:S(2)}, u32[]{:S(2)}) collective-permute-start(bf16[8,128,128]{2,1,0:T(8,128)(2,1)} %bitcast.93), channel_id=1, source_target_pairs={{0,8},{8,16},{16,24},{24,0},{1,9},{9,17},{17,25},{25,1},{2,10},{10... | collective-permute-start | bytes 786440 | tf_op jit(solution)/shard_map/ppermute | solution.py:11
  198.0 69.7 %all-to-all-start.2 = ((s32[8,1,3328]{2,1,0:T(1,128)}), s32[8,1,3328]{2,1,0:T(1,128)S(1)}, u32[]{:S(2)}, u32[]{:S(2)}) async-start(s32[8,1,3328]{2,1,0:T(1,128)} %copy.74), calls=%async_computation.2 | async-start | bytes 212992 | tf_op jit(solution)/shard_map/all_to_all | solution.py:145
  267.7 20.4 %all-to-all-start = ((bf16[8,256,128]{2,1,0:T(8,128)(2,1)}), bf16[8,256,128]{2,1,0:T(8,128)(2,1)S(1)}, u32[]{:S(2)}, u32[]{:S(2)}) async-start(bf16[8,256,128]{2,1,0:T(8,128)(2,1)} %gather_fusion.8), calls=%async_computation | async-start | bytes 1048576 | tf_op jit(solution)/shard_map/all_to_all | solution.py:143
  277.1 15.4 %copy-start.9 = (s32[8,2]{0,1:T(2,128)S(1)}, s32[8,2]{0,1:T(2,128)}, u32[]{:S(2)}) copy-start(s32[8,2]{0,1:T(2,128)} %param.32) | copy-start | bytes 196
  288.1 78.8 %all-to-all-start.3 = ((bf16[8,1536,128]{1,2,0:T(8,128)(2,1)}), bf16[8,1536,128]{1,2,0:T(8,128)(2,1)}, u32[]{:S(2)}, u32[]{:S(2)}) async-start(bf16[8,1536,128]{1,2,0:T(8,128)(2,1)} %gather_fusion.15), calls=%async_computation.3 | async-start | bytes 6291456 | tf_op jit(solution)/shard_map/all_to_all | solution.py:144
  300.6 50.3 %collective-permute-start.4 = (bf16[8,128,128]{2,1,0:T(8,128)(2,1)S(1)}, bf16[8,128,128]{2,1,0:T(8,128)(2,1)S(1)}, u32[]{:S(2)}, u32[]{:S(2)}) collective-permute-start(bf16[8,128,128]{2,1,0:T(8,128)(2,1)S(1)} %bitcast.503), channel_id=1, source_target_pairs={{0,1},{1,2},{2,3},{3,4},{4,5},{5,6},{6,7},{7,0},{8,9},{9,10},{10,1... | collective-permute-start | bytes 786440 | tf_op jit(solution)/shard_map/ppermute | solution.py:11
  306.9 44.7 %collective-permute-start.5 = (bf16[8,128,128]{2,1,0:T(8,128)(2,1)S(1)}, bf16[8,128,128]{2,1,0:T(8,128)(2,1)S(1)}, u32[]{:S(2)}, u32[]{:S(2)}) collective-permute-start(bf16[8,128,128]{2,1,0:T(8,128)(2,1)S(1)} %bitcast.504), channel_id=1, source_target_pairs={{0,8},{8,16},{16,24},{24,0},{1,9},{9,17},{17,25},{25,1},{2,10},{10... | collective-permute-start | bytes 786440 | tf_op jit(solution)/shard_map/ppermute | solution.py:11
where the time goes:
time: 469 us; the launch traced here: 464 us
  matrix products  161 us (34%)
  local copies, waits for them, and re-layouts  144 us (31%)
  waiting for transfers between devices  68.2 us (15%)
  other arithmetic  59.9 us (13%)
  starting transfers between devices  26 us (6%)
    dot_general x192, matrix products, product(): return jnp.dot(left, right, preferred_element_type=jnp.float32)  161 us
    ppermute x6, waiting for transfers between devices, shifted(): lax.ppermute(shard, axis, [(i, (i + by) % devices) for i in range(devices)])  42.6 us
    gather x3, local copies, waits for them, and re-layouts, fetch_ghosts(): along_gy = vertex_state[patch_rows, border_rows[:, 0]]  34.3 us
    gather x3, local copies, waits for them, and re-layouts, fetch_ghosts(): along_gx = vertex_state[patch_rows, border_rows[:, 1]]  26.9 us
    dynamic_update_slice x24, other arithmetic, run_step(): lax.map(lambda pieces: patch_finish(layer_weights, pieces), (vertex_state...  26.1 us
    lt x24, other arithmetic, patch_finish(): live = jnp.arange(edge_total, dtype=jnp.int32) < edge_count  15.3 us
    dynamic_update_slice x48, local copies, waits for them, and re-layouts, run_step(): lax.map(lambda pieces: patch_finish(layer_weights, pieces), (vertex_state...  15 us
    dynamic_slice x24, local copies, waits for them, and re-layouts, run_step(): lax.map(lambda pieces: patch_finish(layer_weights, pieces), (vertex_state...  14.7 us
  transfers between devices with their start and end apart: 10, of which 3 were waited for; matrix products, arithmetic and copies ran while one was open for 54% of the time, Pallas kernels for 0%

commit v1 on v0

v1 whole, which is shorter than its diff:
```python
import functools

import jax
import jax.numpy as jnp
from jax import lax
from jax.experimental import pallas as pl
from jax.experimental.pallas import tpu as pltpu
from jax.sharding import PartitionSpec as P

CHUNK = 256
BF = jnp.bfloat16
F32 = jnp.float32


def product(left, right):
    return jnp.dot(left, right, preferred_element_type=F32)


def normalize(values, scale_row, shift_row):
    center = values - jnp.mean(values, axis=-1, keepdims=True)
    spread = jnp.mean(center * center, axis=-1, keepdims=True)
    return center * lax.rsqrt(spread + 1e-05) * scale_row + shift_row


def ones_where(mask):
    return jnp.where(mask, jnp.ones((), BF), jnp.zeros((), BF))


def spread_ids(row):
    return jnp.transpose(jnp.broadcast_to(row, (128, row.shape[1])))


def one_hot(wide, number, first=0):
    lanes = lax.broadcasted_iota(jnp.int32, wide.shape, 1)
    parts = [
        ones_where(wide == (lanes + (first + start)).astype(F32).astype(BF))
        for start in range(0, number, 128)
    ]
    return jnp.concatenate(parts, axis=1)


def pick_borders(border_ids, vertices):
    wide = spread_ids(border_ids.astype(F32).astype(BF))
    return product(one_hot(wide, vertices.shape[0]), vertices).astype(BF)


def border_kernel(order, v_ref, b_ref, out_ref):
    out_ref[0] = pick_borders(b_ref[0], v_ref[0])


def step_kernel(last, inp, ids, outs, counts, v_ref, e_ref, s_ref, r_ref, b_ref, gy_ref, gx_ref,
                win, wout, bias, gain, *rest):
    if last:
        vo_ref, eo_ref, terms, agg = rest[-4:]
    else:
        vo_ref, eo_ref, bo_ref, terms, agg = rest
    verts = v_ref.shape[1]
    edges = e_ref.shape[1]
    border = gy_ref.shape[1]
    senders_all = verts + 2 * border
    vertices = v_ref[0]
    terms[pl.ds(0, verts)] = product(vertices, win[1]).astype(BF)
    terms[pl.ds(verts, border)] = product(gy_ref[0], win[1]).astype(BF)
    terms[pl.ds(verts + border, border)] = product(gx_ref[0], win[1]).astype(BF)
    terms[pl.ds(senders_all, verts)] = product(vertices, win[2]).astype(BF)
    agg[...] = jnp.zeros_like(agg)
    count = counts[pl.program_id(0)]
    half = senders_all // 2

    def chunk(c, carry):
        base = pl.multiple_of(c * CHUNK, CHUNK)
        rows = pl.ds(base, CHUNK)
        edge = e_ref[0, rows, :]
        sent = (s_ref[0, :, rows] - half).astype(F32).astype(BF)
        lane = base + lax.broadcasted_iota(jnp.int32, (1, CHUNK), 1)
        recv = jnp.where(lane < count, r_ref[0, :, rows], -1).astype(F32).astype(BF)
        hot_s = one_hot(spread_ids(sent), senders_all, -half)
        hot_r = one_hot(spread_ids(recv), verts)
        summed = (
            product(edge, win[0])
            + product(jnp.concatenate([hot_s, hot_r], axis=1), terms[...])
            + bias[0:1, :]
        )
        hidden = jnp.maximum(summed, 0.0).astype(BF)
        update = normalize(product(hidden, wout[0]) + bias[1:2, :], gain[0:1, :], bias[2:3, :])
        row = base + lax.broadcasted_iota(jnp.int32, edge.shape, 0)
        widened = edge.astype(F32)
        fresh = jnp.where(row < count, widened + update, widened).astype(BF)
        eo_ref[0, rows, :] = fresh
        tall = lax.broadcasted_iota(jnp.int32, (verts, CHUNK), 0).astype(F32).astype(BF)
        incoming = ones_where(tall == recv)
        agg[...] += product(incoming, fresh)
        return carry

    live_chunks = (count + (CHUNK - 1)) // CHUNK
    lax.fori_loop(0, live_chunks, chunk, 0)

    def keep(c, carry):
        rows = pl.ds(pl.multiple_of(c * CHUNK, CHUNK), CHUNK)
        eo_ref[0, rows, :] = e_ref[0, rows, :]
        return carry

    lax.fori_loop(live_chunks, edges // CHUNK, keep, 0)

    hidden = product(vertices, win[3]) + product(agg[...].astype(BF), win[4]) + bias[3:4, :]
    hidden = jnp.maximum(hidden, 0.0).astype(BF)
    update = normalize(product(hidden, wout[1]) + bias[4:5, :], gain[1:2, :], bias[5:6, :])
    fresh = (vertices.astype(F32) + update).astype(BF)
    vo_ref[0] = fresh
    if not last:
        bo_ref[0] = pick_borders(b_ref[0], fresh)


def run_borders(order, vertex_state, border_ids):
    patches, verts, width = vertex_state.shape
    wanted = border_ids.shape[2]
    return pl.pallas_call(
        border_kernel,
        out_shape=jax.ShapeDtypeStruct((patches, wanted, width), BF),
        grid_spec=pltpu.PrefetchScalarGridSpec(
            num_scalar_prefetch=1,
            grid=(patches,),
            in_specs=[
                pl.BlockSpec((1, verts, width), lambda p, o: (o[p], 0, 0)),
                pl.BlockSpec((1, 1, wanted), lambda p, o: (o[p], 0, 0)),
            ],
            out_specs=pl.BlockSpec((1, wanted, width), lambda p, o: (p, 0, 0)),
        ),
        cost_estimate=pl.CostEstimate(flops=10**9, bytes_accessed=10**6, transcendentals=0),
    )(order, vertex_state, border_ids)


def run_step(weights, inp, ids, outs, counts, v, e, lists, gy_rows, gx_rows, patches, finals=None):
    senders, receivers, border_ids = lists
    win, wout, bias, gain = weights
    number = counts.shape[0]
    verts, width = v.shape[1:]
    edges = e.shape[1]
    wanted = border_ids.shape[2]
    last = finals is not None

    def at(which):
        return lambda p, *tables: (tables[which][p], 0, 0)

    def own(p, *tables):
        return (p, 0, 0)

    def whole(array):
        return pl.BlockSpec(array.shape, lambda p, *tables: (0,) * array.ndim)

    in_specs = [
        pl.BlockSpec((1, verts, width), at(0)),
        pl.BlockSpec((1, edges, width), at(0)),
        pl.BlockSpec((1, 1, edges), at(1)),
        pl.BlockSpec((1, 1, edges), at(1)),
        pl.BlockSpec((1, 1, wanted), at(1)),
        pl.BlockSpec((1,) + gy_rows.shape[1:], own),
        pl.BlockSpec((1,) + gx_rows.shape[1:], own),
        whole(win), whole(wout), whole(bias), whole(gain),
    ]
    operands = [v, e, senders, receivers, border_ids, gy_rows, gx_rows, win, wout, bias, gain]
    out_specs = [pl.BlockSpec((1, verts, width), at(2)), pl.BlockSpec((1, edges, width), at(2))]
    if last:
        in_specs += [pl.BlockSpec(memory_space=pl.ANY)] * len(finals)
        operands += list(finals)
        shapes = [
            jax.ShapeDtypeStruct((patches, verts, width), BF),
            jax.ShapeDtypeStruct((patches, edges, width), BF),
        ]
        aliases = {4 + 11: 0, 4 + 12: 1} if finals else {}
    else:
        out_specs.append(pl.BlockSpec((1, wanted, width), own))
        shapes = [
            jax.ShapeDtypeStruct((number, verts, width), BF),
            jax.ShapeDtypeStruct((number, edges, width), BF),
            jax.ShapeDtypeStruct((number, wanted, width), BF),
        ]
        aliases = {}
    work = number * edges * width * width * 2 * 11
    return pl.pallas_call(
        functools.partial(step_kernel, last),
        out_shape=shapes,
        grid_spec=pltpu.PrefetchScalarGridSpec(
            num_scalar_prefetch=4,
            grid=(number,),
            in_specs=in_specs,
            out_specs=out_specs,
            scratch_shapes=[
                pltpu.VMEM((verts * 2 + gy_rows.shape[1] * 2, width), BF),
                pltpu.VMEM((verts, width), F32),
            ],
        ),
        input_output_aliases=aliases,
        cost_estimate=pl.CostEstimate(
            flops=work * 4, bytes_accessed=number * edges * width * 4, transcendentals=0
        ),
    )(inp, ids, outs, counts, *operands)


def ring(devices, by):
    return [(i, (i + by) % devices) for i in range(devices)]


def local(vertex_state, edge_state, senders, receivers, counts, border_rows, old_neighbours,
          new_neighbours, new_place, weights_in, weights_out, biases, norm_gains):
    patches, verts, width = vertex_state.shape
    edges = edge_state.shape[1]
    border = border_rows.shape[2]
    size_y = lax.axis_size("gy")
    size_x = lax.axis_size("gx")
    steps = weights_in.shape[0]
    me = lax.axis_index("gy")
    away = (new_place // patches - me) % size_y
    slot = new_place % patches
    local_ids = jnp.arange(patches, dtype=jnp.int32)
    rank = jnp.sum((away[:, None] > away[None, :]).astype(jnp.int32), axis=1)
    placed = rank[None, :] == local_ids[:, None]

    def ranked(values):
        return jnp.sum(jnp.where(placed, values[None, :], 0), axis=1)

    order, slot, counts, away = ranked(local_ids), ranked(slot), ranked(counts), ranked(away)
    lists = (
        senders.reshape(patches, 1, edges),
        receivers.reshape(patches, 1, edges),
        border_rows.reshape(patches, 1, 2 * border),
    )

    def weights_of(step):
        return weights_in[step], weights_out[step], biases[step], norm_gains[step]

    def exchange(rows):
        return (
            lax.ppermute(rows[:, :border], "gy", ring(size_y, 1)),
            lax.ppermute(rows[:, border:], "gx", ring(size_x, 1)),
        )

    first_rows = run_borders(order, vertex_state, lists[2])
    direct = size_y == patches
    finals = ()

    class Group:
        pass

    def settled(tracks):
        group = Group()
        spots = jnp.array(tracks, jnp.int32)
        lo = tracks[0]
        group.ids = order[lo : lo + len(tracks)]
        group.inp = group.ids
        group.counts = counts[lo : lo + len(tracks)]
        group.v, group.e, group.lists = vertex_state, edge_state, lists
        group.ghosts = exchange(first_rows[lo : lo + len(tracks)])
        group.near = jnp.arange(len(tracks), dtype=jnp.int32)
        return group

    def moved(tracks):
        group = Group()
        vs, es, ids, gys, gxs = [], [], [], [], []
        for track in tracks:
            spot = order[track]
            v = lax.dynamic_index_in_dim(vertex_state, spot, 0)
            e = lax.dynamic_index_in_dim(edge_state, spot, 0)
            row = jnp.concatenate(
                [lax.dynamic_index_in_dim(a, spot, 0)[:, 0] for a in lists]
                + [jnp.broadcast_to(counts[track], (1, 64)), jnp.broadcast_to(slot[track], (1, 64))],
                axis=1,
            )
            rows = first_rows[track : track + 1]
            if track:
                v, e, row = (lax.ppermute(a, "gy", ring(size_y, track)) for a in (v, e, row))
            both = [
                (x * size_y + y, (x + 1) % size_x * size_y + (y + track) % size_y)
                for x in range(size_x)
                for y in range(size_y)
            ]
            gys.append(lax.ppermute(rows[:, :border], "gy", ring(size_y, track + 1)) if (track + 1) % size_y else rows[:, :border])
            gxs.append(lax.ppermute(rows[:, border:], ("gx", "gy"), both))
            vs.append(v)
            es.append(e)
            ids.append(row)
        group.v = jnp.concatenate(vs)
        group.e = jnp.concatenate(es)
        row = jnp.concatenate(ids)
        group.ghosts = (jnp.concatenate(gys), jnp.concatenate(gxs))
        group.lists = tuple(
            row[:, None, a:b]
            for a, b in ((0, edges), (edges, 2 * edges), (2 * edges, 2 * edges + 2 * border))
        )
        end = 2 * edges + 2 * border
        group.counts = row[:, end]
        group.slots = row[:, end + 64]
        group.near = jnp.arange(len(tracks), dtype=jnp.int32)
        group.inp = group.ids = group.near
        return group

    def advance(group, step, finals=None):
        outs = group.near if finals is None else group.slots
        got = run_step(weights_of(step), group.inp, group.ids, outs, group.counts, group.v, group.e,
                       group.lists, *group.ghosts, patches, finals=finals)
        if finals is not None:
            return got
        group.v, group.e, rows = got
        group.inp = group.near
        if step < steps - 1:
            group.ghosts = exchange(rows)

    if direct:
        half = patches // 2
        far = [t for t in range(patches // 4, patches // 4 + half)]
        near = [t for t in range(patches) if t not in far]
        sets = [far[: half // 2], far[half // 2 :]]
        late = [near[: half // 2], near[half // 2 :]]
        landing = {t: lax.ppermute(jnp.broadcast_to(slot[t], (1, 128)), "gy", ring(size_y, t)) for t in far}
        late_groups = [moved(tracks) for tracks in late]
        early = [settled(tracks) for tracks in sets]
        for step in range(steps):
            for group in early:
                advance(group, step)
        arrivals = []
        for group, tracks in zip(early, sets):
            for i, track in enumerate(tracks):
                arrivals.append((
                    landing[track][0, 0],
                    lax.ppermute(group.v[i : i + 1], "gy", ring(size_y, track)),
                    lax.ppermute(group.e[i : i + 1], "gy", ring(size_y, track)),
                ))
        for step in range(steps - 1):
            for group in late_groups:
                advance(group, step)
        for group in late_groups:
            finals = advance(group, steps - 1, finals)
        vertex_out, edge_out = finals
        for where, v, e in arrivals:
            vertex_out = lax.dynamic_update_slice(vertex_out, v, (where, 0, 0))
            edge_out = lax.dynamic_update_slice(edge_out, e, (where, 0, 0))
        return vertex_out, edge_out

    half = patches // 2
    groups = [settled(list(range(half))), settled(list(range(half, patches)))]
    for step in range(steps):
        for group in groups:
            advance(group, step)
    vertex_state = jnp.concatenate([g.v for g in groups])
    edge_state = jnp.concatenate([g.e for g in groups])
    capacity = (patches + size_y - 1) // size_y
    target = (away + me) % size_y
    earlier = (target[:, None] == target[None, :]) & (local_ids[:, None] > local_ids[None, :])
    place = target * capacity + jnp.sum(earlier.astype(jnp.int32), axis=1)
    box = jnp.arange(size_y * capacity, dtype=jnp.int32)
    filled = place[None, :] == box[:, None]
    source = jnp.sum(jnp.where(filled, local_ids[None, :], 0), axis=1)
    header = jnp.where(jnp.any(filled, axis=1), slot[source], -1)
    header = jnp.broadcast_to(header[:, None], (box.shape[0], 2))
    arrived = [
        lax.all_to_all(a, "gy", split_axis=0, concat_axis=0, tiled=True)
        for a in (vertex_state[source], edge_state[source], header)
    ]
    landing = arrived[2][:, 0]
    chosen = jnp.sum(jnp.where(landing[None, :] == local_ids[:, None], box[None, :], 0), axis=1)
    return arrived[0][chosen], arrived[1][chosen]


def solution(mesh):
    held = P(("gx", "gy"))
    return jax.shard_map(
        local,
        mesh=mesh,
        in_specs=(held,) * 9 + (P(),) * 4,
        out_specs=(held, held),
        check_vma=False,
    )
```

time: 469 us -> 354 us (0.75)
  the two profiles are of different devices: /device:TPU:0 before, /device:TPU:8 now
where the time goes in v1:
time: 354 us; the launch traced here: 353 us
  Pallas kernels  165 us (47%)
  local copies, waits for them, and re-layouts  56.4 us (16%)
  waiting for transfers between devices  54.8 us (15%)
  starting transfers between devices  50.5 us (14%)
  other arithmetic  12.8 us (4%)
  between operations  12.8 us (4%)
    pallas_call x12, Pallas kernels, run_step(): pl.pallas_call(functools.partial(step_kernel, last), out_shape=shapes, gr...  159 us
    ppermute x4, waiting for transfers between devices, local(): lax.ppermute(group.e[i:i + 1], 'gy', ring(size_y, track))  35.3 us
    ppermute x9, starting transfers between devices, moved(): lax.ppermute(a, 'gy', ring(size_y, track))  8.92 us
    slice x9, local copies, waits for them, and re-layouts, exchange(): rows[:, border:]  8.69 us
    ppermute x10, starting transfers between devices, exchange(): lax.ppermute(rows[:, border:], 'gx', ring(size_x, 1))  8.38 us
    ppermute x10, starting transfers between devices, exchange(): lax.ppermute(rows[:, :border], 'gy', ring(size_y, 1))  8.32 us
    ppermute x4, starting transfers between devices, local(): lax.ppermute(group.v[i:i + 1], 'gy', ring(size_y, track))  8.15 us
    ppermute x10, waiting for transfers between devices, exchange(): lax.ppermute(rows[:, :border], 'gy', ring(size_y, 1))  7.39 us
  transfers between devices with their start and end apart: 48, of which 13 were waited for; matrix products, arithmetic and copies ran while one was open for 17% of the time, Pallas kernels for 47%

profile of v1, /device:TPU:8, one launch (start us, length us, event | category | flops | bytes accessed | tf_op | source)
XLA Modules:
  0.0 352.7 jit_solution(15186298006034639080)
XLA Ops:
  12.2 1.7 constant_dynamic-slice_fusion.8
  18.6 3.5 collective-permute-start
  22.1 1.6 constant_dynamic-slice_fusion.3
  26.5 6.3 %shard_map.122 = bf16[8,256,128]{2,1,0:T(8,128)(2,1)} custom-call(s32[8]{0:T(128)} %copy-done.10, bf16[8,256,128]{2,1,0:T(8,128)(2,1)} %v_ref.5, s32[8,1,256]{2,1,0:T(1,128)} %bitcast.66), custom_call_target="tpu_custom_call" | custom-call | flops 1000000000 | bytes 1000000 | tf_op jit(solution)/shard_map/pallas_call | solution.py:117
  32.8 1.6 fusion.16
  34.5 1.6 fusion.15
  46.7 3.9 %collective-permute-start.41 = (s32[1,128]{1,0:T(1,128)S(1)}, s32[1,128]{1,0:T(1,128)S(1)}, u32[]{:S(2)}, u32[]{:S(2)}) collective-permute-start(s32[1,128]{1,0:T(1,128)S(1)} %broadcast_in_dim.105), channel_id=1, source_target_pairs={{0,4},{1,5},{2,6},{3,7},{4,0},{5,1},{6,2},{7,3},{8,12},{9,13},{10,... | collective-permute-start | bytes 1544 | tf_op jit(solution)/shard_map/ppermute | solution.py:314
  52.4 1.4 collective-permute-start.43
  55.4 1.5 collective-permute-start.5
  60.2 2.0 collective-permute-done.13
  66.7 1.5 add_reduce_fusion.2
  68.9 4.4 %collective-permute-start.7 = (bf16[1,128,128]{2,1,0:T(8,128)(2,1)}, bf16[1,128,128]{2,1,0:T(8,128)(2,1)S(1)}, u32[]{:S(2)}, u32[]{:S(2)}) collective-permute-start(bf16[1,128,128]{2,1,0:T(8,128)(2,1)} %get-tuple-element.90), channel_id=1, source_target_pairs={{0,14},{1,15},{2,8},{3,9},{4,10},{5,11},{6,12},{7,13},{8,22},{9,23... | collective-permute-start | bytes 98312 | tf_op jit(solution)/shard_map/ppermute | solution.py:278
  73.3 1.4 pad_maximum_fusion.4.gy_ref
  75.9 3.0 collective-permute-done.17
  81.3 2.9 collective-permute-done.19
  85.8 2.3 collective-permute-done.24.gy_ref
  88.1 2.1 collective-permute-done.25.gx_ref
  90.9 14.6 %shard_map.129 = (bf16[2,256,128]{2,1,0:T(8,128)(2,1)}, bf16[2,1536,128]{2,1,0:T(8,128)(2,1)}, bf16[2,256,128]{2,1,0:T(8,128)(2,1)}) custom-call(s32[2]{0:T(128)} %get-tuple-element.171.inp.ids, s32[2]{0:T(128)} %get-tuple-element.171.inp.ids, s32[2]{0:T(128)} %iota.71.outs, s32[2]{0:T(128)} %get-tuple-element.154.counts, bf16[8,256,128]{2,1,0:T(8,128)(2,1)} %v_ref.5, ...), custom_call_target="tpu_custom_call" | custom-call | flops 4429185024 | bytes 1572864 | tf_op jit(solution)/shard_map/pallas_call | solution.py:180
  106.4 2.7 collective-permute-start.4
  109.7 13.8 %shard_map.132 = (bf16[2,256,128]{2,1,0:T(8,128)(2,1)}, bf16[2,1536,128]{2,1,0:T(8,128)(2,1)}, bf16[2,256,128]{2,1,0:T(8,128)(2,1)}) custom-call(s32[2]{0:T(128)} %get-tuple-element.172.inp.ids, s32[2]{0:T(128)} %get-tuple-element.172.inp.ids, s32[2]{0:T(128)} %iota.74.outs, s32[2]{0:T(128)} %get-tuple-element.153.counts, bf16[8,256,128]{2,1,0:T(8,128)(2,1)} %v_ref.5, ...), custom_call_target="tpu_custom_call" | custom-call | flops 4429185024 | bytes 1572864 | tf_op jit(solution)/shard_map/pallas_call | solution.py:180
  124.9 1.5 pad_maximum_fusion.2.v_ref
  127.5 5.0 %collective-permute-done.26.gy_ref = bf16[2,128,128]{2,1,0:T(8,128)(2,1)S(1)} collective-permute-done((bf16[2,128,128]{2,1,0:T(8,128)(2,1)S(1)}, bf16[2,128,128]{2,1,0:T(8,128)(2,1)S(1)}, u32[]{:S(2)}, u32[]{:S(2)}) %collective-permute-start.26) | collective-permute-done | bytes 65568 | tf_op jit(solution)/shard_map/ppermute | solution.py:234
  134.0 14.5 %shard_map.130 = (bf16[2,256,128]{2,1,0:T(8,128)(2,1)}, bf16[2,1536,128]{2,1,0:T(8,128)(2,1)}, bf16[2,256,128]{2,1,0:T(8,128)(2,1)}) custom-call(s32[2]{0:T(128)} %iota.70.inp.outs, s32[2]{0:T(128)} %get-tuple-element.171.inp.ids, s32[2]{0:T(128)} %iota.70.inp.outs, s32[2]{0:T(128)} %get-tuple-element.154.counts, ...), custom_call_target="tpu_custom_call" | custom-call | flops 4429185024 | bytes 1572864 | tf_op jit(solution)/shard_map/pallas_call | solution.py:180
  151.1 13.7 %shard_map.133 = (bf16[2,256,128]{2,1,0:T(8,128)(2,1)}, bf16[2,1536,128]{2,1,0:T(8,128)(2,1)}, bf16[2,256,128]{2,1,0:T(8,128)(2,1)}) custom-call(s32[2]{0:T(128)} %iota.73.inp.outs, s32[2]{0:T(128)} %get-tuple-element.172.inp.ids, s32[2]{0:T(128)} %iota.73.inp.outs, s32[2]{0:T(128)} %get-tuple-element.153.counts, ...), custom_call_target="tpu_custom_call" | custom-call | flops 4429185024 | bytes 1572864 | tf_op jit(solution)/shard_map/pallas_call | solution.py:180
  165.7 2.3 collective-permute-start.38
  168.6 14.5 %shard_map.131 = (bf16[2,256,128]{2,1,0:T(8,128)(2,1)}, bf16[2,1536,128]{2,1,0:T(8,128)(2,1)}, bf16[2,256,128]{2,1,0:T(8,128)(2,1)}) custom-call(s32[2]{0:T(128)} %iota.69.inp.outs, s32[2]{0:T(128)} %get-tuple-element.171.inp.ids, s32[2]{0:T(128)} %iota.69.inp.outs, s32[2]{0:T(128)} %get-tuple-element.154.counts, ...), custom_call_target="tpu_custom_call" | custom-call | flops 4429185024 | bytes 1572864 | tf_op jit(solution)/shard_map/pallas_call | solution.py:180
  183.1 1.5 fusion.20
  185.4 3.1 collective-permute-start.32
  189.0 13.8 %shard_map.134 = (bf16[2,256,128]{2,1,0:T(8,128)(2,1)}, bf16[2,1536,128]{2,1,0:T(8,128)(2,1)}, bf16[2,256,128]{2,1,0:T(8,128)(2,1)}) custom-call(s32[2]{0:T(128)} %iota.72.inp.outs, s32[2]{0:T(128)} %get-tuple-element.172.inp.ids, s32[2]{0:T(128)} %iota.72.inp.outs, s32[2]{0:T(128)} %get-tuple-element.153.counts, ...), custom_call_target="tpu_custom_call" | custom-call | flops 4429185024 | bytes 1572864 | tf_op jit(solution)/shard_map/pallas_call | solution.py:180
  202.8 1.5 fusion.17
  207.1 12.9 %shard_map.125 = (bf16[2,256,128]{2,1,0:T(8,128)(2,1)}, bf16[2,1536,128]{2,1,0:T(8,128)(2,1)}, bf16[2,256,128]{2,1,0:T(8,128)(2,1)}) custom-call(s32[2]{0:T(128)} %iota.68.inp.ids.outs, s32[2]{0:T(128)} %iota.68.inp.ids.outs, s32[2]{0:T(128)} %iota.68.inp.ids.outs, s32[2]{0:T(128)} %get-tuple-element.66.counts, ...), custom_call_target="tpu_custom_call" | custom-call | flops 4429185024 | bytes 1572864 | tf_op jit(solution)/shard_map/pallas_call | solution.py:180
  222.6 12.1 %shard_map.123 = (bf16[2,256,128]{2,1,0:T(8,128)(2,1)}, bf16[2,1536,128]{2,1,0:T(8,128)(2,1)}, bf16[2,256,128]{2,1,0:T(8,128)(2,1)}) custom-call(s32[2]{0:T(128)} %iota.65.inp.ids.outs, s32[2]{0:T(128)} %iota.65.inp.ids.outs, s32[2]{0:T(128)} %iota.65.inp.ids.outs, s32[2]{0:T(128)} %get-tuple-element.68.counts, ...), custom_call_target="tpu_custom_call" | custom-call | flops 4429185024 | bytes 1572864 | tf_op jit(solution)/shard_map/pallas_call | solution.py:180
  235.5 3.9 %collective-permute-start.9 = (bf16[2,128,128]{2,1,0:T(8,128)(2,1)S(1)}, bf16[2,128,128]{2,1,0:T(8,128)(2,1)S(1)}, u32[]{:S(2)}, u32[]{:S(2)}) collective-permute-start(bf16[2,128,128]{2,1,0:T(8,128)(2,1)S(1)} %get-tuple-element.122), channel_id=1, source_target_pairs={{0,1},{1,2},{2,3},{3,4},{4,5},{5,6},{6,7},{7,0},{8,9},{9,10},{10,1... | collective-permute-start | bytes 196616 | tf_op jit(solution)/shard_map/ppermute | solution.py:234
  239.4 1.9 collective-permute-start.10
  242.0 12.9 %shard_map.126 = (bf16[2,256,128]{2,1,0:T(8,128)(2,1)}, bf16[2,1536,128]{2,1,0:T(8,128)(2,1)}, bf16[2,256,128]{2,1,0:T(8,128)(2,1)}) custom-call(s32[2]{0:T(128)} %iota.67.inp.ids.outs, s32[2]{0:T(128)} %iota.67.inp.ids.outs, s32[2]{0:T(128)} %iota.67.inp.ids.outs, s32[2]{0:T(128)} %get-tuple-element.66.counts, ...), custom_call_target="tpu_custom_call" | custom-call | flops 4429185024 | bytes 1572864 | tf_op jit(solution)/shard_map/pallas_call | solution.py:180
  257.3 12.1 %shard_map.124 = (bf16[2,256,128]{2,1,0:T(8,128)(2,1)}, bf16[2,1536,128]{2,1,0:T(8,128)(2,1)}, bf16[2,256,128]{2,1,0:T(8,128)(2,1)}) custom-call(s32[2]{0:T(128)} %iota.64.inp.ids.outs, s32[2]{0:T(128)} %iota.64.inp.ids.outs, s32[2]{0:T(128)} %iota.64.inp.ids.outs, s32[2]{0:T(128)} %get-tuple-element.68.counts, ...), custom_call_target="tpu_custom_call" | custom-call | flops 4429185024 | bytes 1572864 | tf_op jit(solution)/shard_map/pallas_call | solution.py:180
  270.3 1.9 collective-permute-start.11
  272.2 2.8 collective-permute-start.12
  275.5 12.6 %shard_map.127 = (bf16[8,256,128]{2,1,0:T(8,128)(2,1)}, bf16[8,1536,128]{2,1,0:T(8,128)(2,1)}) custom-call(s32[2]{0:T(128)} %iota.66.inp.ids, s32[2]{0:T(128)} %iota.66.inp.ids, s32[2]{0:T(128)} %get-tuple-element.67.outs, s32[2]{0:T(128)} %get-tuple-element.66.counts, bf16[2,256,128]{2,1,0:T(8,128)(2,1)} %get-tuple-element.43.v_ref, ...), custom_call_target="tpu_custom_call" | custom-call | flops 4429185024 | bytes 1572864 | tf_op jit(solution)/shard_map/pallas_call | solution.py:180
  288.1 4.2 %collective-permute-start.42 = (bf16[1,256,128]{2,1,0:T(8,128)(2,1)S(1)}, bf16[1,256,128]{2,1,0:T(8,128)(2,1)S(1)}, u32[]{:S(2)}, u32[]{:S(2)}) collective-permute-start(bf16[1,256,128]{2,1,0:T(8,128)(2,1)S(1)} %copy-done.8), channel_id=1, source_target_pairs={{0,5},{1,6},{2,7},{3,0},{4,1},{5,2},{6,3},{7,4},{8,13},{9,14},{10,... | collective-permute-start | bytes 196616 | tf_op jit(solution)/shard_map/ppermute | solution.py:325
  292.9 11.6 %shard_map.128 = (bf16[8,256,128]{2,1,0:T(8,128)(2,1)}, bf16[8,1536,128]{2,1,0:T(8,128)(2,1)}) custom-call(s32[2]{0:T(128)} %iota.63.inp.ids, s32[2]{0:T(128)} %iota.63.inp.ids, s32[2]{0:T(128)} %get-tuple-element.69.outs, s32[2]{0:T(128)} %get-tuple-element.68.counts, ...), custom_call_target="tpu_custom_call", output_to_operand_aliasing={{0}: (15, {}), {1}: (16, {})} | custom-call | flops 4429185024 | bytes 1572864 | tf_op jit(solution)/shard_map/pallas_call | solution.py:180
  305.7 1.5 constant_dynamic-update-slice_fusion.7
  307.1 3.1 collective-permute-start.46
  310.2 1.5 constant_dynamic-update-slice_fusion.6
  312.2 1.5 constant_dynamic-update-slice_fusion.5
  315.0 21.2 %collective-permute-done.45 = bf16[1,1536,128]{2,1,0:T(8,128)(2,1)S(1)} collective-permute-done((bf16[1,1536,128]{2,1,0:T(8,128)(2,1)S(1)}, bf16[1,1536,128]{2,1,0:T(8,128)(2,1)S(1)}, u32[]{:S(2)}, u32[]{:S(2)}) %collective-permute-start.45) | collective-permute-done | bytes 393248 | tf_op jit(solution)/shard_map/ppermute | solution.py:326
  337.0 7.0 %collective-permute-done.46 = bf16[1,1536,128]{2,1,0:T(8,128)(2,1)S(1)} collective-permute-done((bf16[1,1536,128]{2,1,0:T(8,128)(2,1)S(1)}, bf16[1,1536,128]{2,1,0:T(8,128)(2,1)S(1)}, u32[]{:S(2)}, u32[]{:S(2)}) %collective-permute-start.46) | collective-permute-done | bytes 393248 | tf_op jit(solution)/shard_map/ppermute | solution.py:326
  344.8 7.1 %collective-permute-done.47 = bf16[1,1536,128]{2,1,0:T(8,128)(2,1)S(1)} collective-permute-done((bf16[1,1536,128]{2,1,0:T(8,128)(2,1)S(1)}, bf16[1,1536,128]{2,1,0:T(8,128)(2,1)S(1)}, u32[]{:S(2)}, u32[]{:S(2)}) %collective-permute-start.47) | collective-permute-done | bytes 393248 | tf_op jit(solution)/shard_map/ppermute | solution.py:326
  (219 shorter events, 62.9 us)
Async XLA Ops:
  16.7 41.6 %collective-permute-start.1 = (s32[1,3456]{1,0:T(1,128)}, s32[1,3456]{1,0:T(1,128)S(1)}, u32[]{:S(2)}, u32[]{:S(2)}) collective-permute-start(s32[1,3456]{1,0:T(1,128)} %concatenate.43), channel_id=1, source_target_pairs={{0,7},{1,0},{2,1},{3,2},{4,3},{5,4},{6,5},{7,6},{8,15},{9,8},{10,9... | collective-permute-start | bytes 41480 | tf_op jit(solution)/shard_map/ppermute | solution.py:271
  18.6 39.8 %collective-permute-start = (s32[1,3456]{1,0:T(1,128)}, s32[1,3456]{1,0:T(1,128)}, u32[]{:S(2)}, u32[]{:S(2)}) collective-permute-start(s32[1,3456]{1,0:T(1,128)} %concatenate.42), channel_id=1, source_target_pairs={{0,6},{1,7},{2,0},{3,1},{4,2},{5,3},{6,4},{7,5},{8,14},{9,15},{10,... | collective-permute-start | bytes 41480 | tf_op jit(solution)/shard_map/ppermute | solution.py:271
  23.7 100.7 %collective-permute-start.3 = (bf16[1,256,128]{2,1,0:T(8,128)(2,1)}, bf16[1,256,128]{2,1,0:T(8,128)(2,1)}, u32[]{:S(2)}, u32[]{:S(2)}) collective-permute-start(bf16[1,256,128]{2,1,0:T(8,128)(2,1)} %get-tuple-element.95), channel_id=1, source_target_pairs={{0,7},{1,0},{2,1},{3,2},{4,3},{5,4},{6,5},{7,6},{8,15},{9,8},{10,9... | collective-permute-start | bytes 196616 | tf_op jit(solution)/shard_map/ppermute | solution.py:271
  25.3 20.7 %collective-permute-start.31 = (s32[1,128]{1,0:T(1,128)}, s32[1,128]{1,0:T(1,128)}, u32[]{:S(2)}, u32[]{:S(2)}) collective-permute-start(s32[1,128]{1,0:T(1,128)} %broadcast_in_dim.103), channel_id=1, source_target_pairs={{0,2},{1,3},{2,4},{3,5},{4,6},{5,7},{6,0},{7,1},{8,10},{9,11},{10,... | collective-permute-start | bytes 1544 | tf_op jit(solution)/shard_map/ppermute | solution.py:314
  26.5 25.3 %collective-permute-start.33 = (s32[1,128]{1,0:T(1,128)}, s32[1,128]{1,0:T(1,128)}, u32[]{:S(2)}, u32[]{:S(2)}) collective-permute-start(s32[1,128]{1,0:T(1,128)} %broadcast_in_dim.104), channel_id=1, source_target_pairs={{0,3},{1,4},{2,5},{3,6},{4,7},{5,0},{6,1},{7,2},{8,11},{9,12},{10,... | collective-permute-start | bytes 1544 | tf_op jit(solution)/shard_map/ppermute | solution.py:314
  46.7 8.3 %collective-permute-start.41 = (s32[1,128]{1,0:T(1,128)S(1)}, s32[1,128]{1,0:T(1,128)S(1)}, u32[]{:S(2)}, u32[]{:S(2)}) collective-permute-start(s32[1,128]{1,0:T(1,128)S(1)} %broadcast_in_dim.105), channel_id=1, source_target_pairs={{0,4},{1,5},{2,6},{3,7},{4,0},{5,1},{6,2},{7,3},{8,12},{9,13},{10,... | collective-permute-start | bytes 1544 | tf_op jit(solution)/shard_map/ppermute | solution.py:314
  52.4 3.0 collective-permute-start.43
  55.0 69.8 %collective-permute-start.2 = (bf16[1,256,128]{2,1,0:T(8,128)(2,1)}, bf16[1,256,128]{2,1,0:T(8,128)(2,1)S(1)}, u32[]{:S(2)}, u32[]{:S(2)}) collective-permute-start(bf16[1,256,128]{2,1,0:T(8,128)(2,1)} %get-tuple-element.96), channel_id=1, source_target_pairs={{0,6},{1,7},{2,0},{3,1},{4,2},{5,3},{6,4},{7,5},{8,14},{9,15},{10,... | collective-permute-start | bytes 196616 | tf_op jit(solution)/shard_map/ppermute | solution.py:271
  55.4 165.5 %collective-permute-start.5 = (bf16[1,1536,128]{2,1,0:T(8,128)(2,1)}, bf16[1,1536,128]{2,1,0:T(8,128)(2,1)S(1)}, u32[]{:S(2)}, u32[]{:S(2)}) collective-permute-start(bf16[1,1536,128]{2,1,0:T(8,128)(2,1)} %get-tuple-element.75), channel_id=1, source_target_pairs={{0,7},{1,0},{2,1},{3,2},{4,3},{5,4},{6,5},{7,6},{8,15},{9,8},{10,9... | collective-permute-start | bytes 1179656 | tf_op jit(solution)/shard_map/ppermute | solution.py:271
  58.3 10.6 %collective-permute-start.6 = (bf16[1,128,128]{2,1,0:T(8,128)(2,1)}, bf16[1,128,128]{2,1,0:T(8,128)(2,1)S(1)}, u32[]{:S(2)}, u32[]{:S(2)}) collective-permute-start(bf16[1,128,128]{2,1,0:T(8,128)(2,1)} %get-tuple-element.92), channel_id=1, source_target_pairs={{0,7},{1,0},{2,1},{3,2},{4,3},{5,4},{6,5},{7,6},{8,15},{9,8},{10,9... | collective-permute-start | bytes 98312 | tf_op jit(solution)/shard_map/ppermute | solution.py:277
  58.4 3.8 %collective-permute-start.13 = (s32[1,3456]{1,0:T(1,128)S(1)}, s32[1,3456]{1,0:T(1,128)S(1)}, u32[]{:S(2)}, u32[]{:S(2)}) collective-permute-start(s32[1,3456]{1,0:T(1,128)S(1)} %concatenate.50), channel_id=1, source_target_pairs={{0,1},{1,2},{2,3},{3,4},{4,5},{5,6},{6,7},{7,0},{8,9},{9,10},{10,1... | collective-permute-start | bytes 41480 | tf_op jit(solution)/shard_map/ppermute | solution.py:271
  62.2 12.5 %collective-permute-start.8 = (bf16[1,128,128]{2,1,0:T(8,128)(2,1)}, bf16[1,128,128]{2,1,0:T(8,128)(2,1)S(1)}, u32[]{:S(2)}, u32[]{:S(2)}) collective-permute-start(bf16[1,128,128]{2,1,0:T(8,128)(2,1)} %get-tuple-element.89), channel_id=1, source_target_pairs={{0,15},{1,8},{2,9},{3,10},{4,11},{5,12},{6,13},{7,14},{8,23},{9,16... | collective-permute-start | bytes 98312 | tf_op jit(solution)/shard_map/ppermute | solution.py:278
  68.9 6.3 %collective-permute-start.7 = (bf16[1,128,128]{2,1,0:T(8,128)(2,1)}, bf16[1,128,128]{2,1,0:T(8,128)(2,1)S(1)}, u32[]{:S(2)}, u32[]{:S(2)}) collective-permute-start(bf16[1,128,128]{2,1,0:T(8,128)(2,1)} %get-tuple-element.90), channel_id=1, source_target_pairs={{0,14},{1,15},{2,8},{3,9},{4,10},{5,11},{6,12},{7,13},{8,22},{9,23... | collective-permute-start | bytes 98312 | tf_op jit(solution)/shard_map/ppermute | solution.py:278
  74.7 4.1 %collective-permute-start.17 = (bf16[1,128,128]{2,1,0:T(8,128)(2,1)}, bf16[1,128,128]{2,1,0:T(8,128)(2,1)S(1)}, u32[]{:S(2)}, u32[]{:S(2)}) collective-permute-start(bf16[1,128,128]{2,1,0:T(8,128)(2,1)} %get-tuple-element.87), channel_id=1, source_target_pairs={{0,2},{1,3},{2,4},{3,5},{4,6},{5,7},{6,0},{7,1},{8,10},{9,11},{10,... | collective-permute-start | bytes 98312 | tf_op jit(solution)/shard_map/ppermute | solution.py:277
  75.2 4.5 %collective-permute-start.16 = (bf16[1,128,128]{2,1,0:T(8,128)(2,1)}, bf16[1,128,128]{2,1,0:T(8,128)(2,1)S(1)}, u32[]{:S(2)}, u32[]{:S(2)}) collective-permute-start(bf16[1,128,128]{2,1,0:T(8,128)(2,1)} %get-tuple-element.88), channel_id=1, source_target_pairs={{0,1},{1,2},{2,3},{3,4},{4,5},{5,6},{6,7},{7,0},{8,9},{9,10},{10,1... | collective-permute-start | bytes 98312 | tf_op jit(solution)/shard_map/ppermute | solution.py:277
  78.8 5.4 %collective-permute-start.19 = (bf16[1,128,128]{2,1,0:T(8,128)(2,1)}, bf16[1,128,128]{2,1,0:T(8,128)(2,1)S(1)}, u32[]{:S(2)}, u32[]{:S(2)}) collective-permute-start(bf16[1,128,128]{2,1,0:T(8,128)(2,1)} %get-tuple-element.86), channel_id=1, source_target_pairs={{0,9},{1,10},{2,11},{3,12},{4,13},{5,14},{6,15},{7,8},{8,17},{9,18... | collective-permute-start | bytes 98312 | tf_op jit(solution)/shard_map/ppermute | solution.py:278
  79.8 5.1 %collective-permute-start.18 = (bf16[1,128,128]{2,1,0:T(8,128)(2,1)}, bf16[1,128,128]{2,1,0:T(8,128)(2,1)S(1)}, u32[]{:S(2)}, u32[]{:S(2)}) collective-permute-start(bf16[1,128,128]{2,1,0:T(8,128)(2,1)} %get-tuple-element.85), channel_id=1, source_target_pairs={{0,8},{1,9},{2,10},{3,11},{4,12},{5,13},{6,14},{7,15},{8,16},{9,17... | collective-permute-start | bytes 98312 | tf_op jit(solution)/shard_map/ppermute | solution.py:278
  84.2 3.9 %collective-permute-start.24 = (bf16[2,128,128]{2,1,0:T(8,128)(2,1)}, bf16[2,128,128]{2,1,0:T(8,128)(2,1)S(1)}, u32[]{:S(2)}, u32[]{:S(2)}) collective-permute-start(bf16[2,128,128]{2,1,0:T(8,128)(2,1)} %get-tuple-element.84), channel_id=1, source_target_pairs={{0,1},{1,2},{2,3},{3,4},{4,5},{5,6},{6,7},{7,0},{8,9},{9,10},{10,1... | collective-permute-start | bytes 196616 | tf_op jit(solution)/shard_map/ppermute | solution.py:234
  84.9 5.4 %collective-permute-start.25 = (bf16[2,128,128]{2,1,0:T(8,128)(2,1)}, bf16[2,128,128]{2,1,0:T(8,128)(2,1)S(1)}, u32[]{:S(2)}, u32[]{:S(2)}) collective-permute-start(bf16[2,128,128]{2,1,0:T(8,128)(2,1)} %get-tuple-element.83), channel_id=1, source_target_pairs={{0,8},{8,16},{16,24},{24,0},{1,9},{9,17},{17,25},{25,1},{2,10},{10... | collective-permute-start | bytes 196616 | tf_op jit(solution)/shard_map/ppermute | solution.py:235
  88.1 18.3 %collective-permute-start.34 = (bf16[2,128,128]{2,1,0:T(8,128)(2,1)}, bf16[2,128,128]{2,1,0:T(8,128)(2,1)S(1)}, u32[]{:S(2)}, u32[]{:S(2)}) collective-permute-start(bf16[2,128,128]{2,1,0:T(8,128)(2,1)} %get-tuple-element.82), channel_id=1, source_target_pairs={{0,1},{1,2},{2,3},{3,4},{4,5},{5,6},{6,7},{7,0},{8,9},{9,10},{10,1... | collective-permute-start | bytes 196616 | tf_op jit(solution)/shard_map/ppermute | solution.py:234
  90.3 18.8 %collective-permute-start.35 = (bf16[2,128,128]{2,1,0:T(8,128)(2,1)}, bf16[2,128,128]{2,1,0:T(8,128)(2,1)S(1)}, u32[]{:S(2)}, u32[]{:S(2)}) collective-permute-start(bf16[2,128,128]{2,1,0:T(8,128)(2,1)} %get-tuple-element.81), channel_id=1, source_target_pairs={{0,8},{8,16},{16,24},{24,0},{1,9},{9,17},{17,25},{25,1},{2,10},{10... | collective-permute-start | bytes 196616 | tf_op jit(solution)/shard_map/ppermute | solution.py:235
  106.4 114.6 %collective-permute-start.4 = (bf16[1,1536,128]{2,1,0:T(8,128)(2,1)S(1)}, bf16[1,1536,128]{2,1,0:T(8,128)(2,1)S(1)}, u32[]{:S(2)}, u32[]{:S(2)}) collective-permute-start(bf16[1,1536,128]{2,1,0:T(8,128)(2,1)S(1)} %copy-done.3), channel_id=1, source_target_pairs={{0,6},{1,7},{2,0},{3,1},{4,2},{5,3},{6,4},{7,5},{8,14},{9,15},{10,... | collective-permute-start | bytes 1179656 | tf_op jit(solution)/shard_map/ppermute | solution.py:271
  109.1 17.3 %collective-permute-start.14 = (bf16[1,256,128]{2,1,0:T(8,128)(2,1)S(1)}, bf16[1,256,128]{2,1,0:T(8,128)(2,1)S(1)}, u32[]{:S(2)}, u32[]{:S(2)}) collective-permute-start(bf16[1,256,128]{2,1,0:T(8,128)(2,1)S(1)} %copy-done.9), channel_id=1, source_target_pairs={{0,1},{1,2},{2,3},{3,4},{4,5},{5,6},{6,7},{7,0},{8,9},{9,10},{10,1... | collective-permute-start | bytes 196616 | tf_op jit(solution)/shard_map/ppermute | solution.py:271
  124.4 81.2 %collective-permute-start.15 = (bf16[1,1536,128]{2,1,0:T(8,128)(2,1)}, bf16[1,1536,128]{2,1,0:T(8,128)(2,1)S(1)}, u32[]{:S(2)}, u32[]{:S(2)}) collective-permute-start(bf16[1,1536,128]{2,1,0:T(8,128)(2,1)} %get-tuple-element.74), channel_id=1, source_target_pairs={{0,1},{1,2},{2,3},{3,4},{4,5},{5,6},{6,7},{7,0},{8,9},{9,10},{10,1... | collective-permute-start | bytes 1179656 | tf_op jit(solution)/shard_map/ppermute | solution.py:271
  124.8 7.8 %collective-permute-start.26 = (bf16[2,128,128]{2,1,0:T(8,128)(2,1)S(1)}, bf16[2,128,128]{2,1,0:T(8,128)(2,1)S(1)}, u32[]{:S(2)}, u32[]{:S(2)}) collective-permute-start(bf16[2,128,128]{2,1,0:T(8,128)(2,1)S(1)} %get-tuple-element.114), channel_id=1, source_target_pairs={{0,1},{1,2},{2,3},{3,4},{4,5},{5,6},{6,7},{7,0},{8,9},{9,10},{10,1... | collective-permute-start | bytes 196616 | tf_op jit(solution)/shard_map/ppermute | solution.py:234
  126.4 6.2 %collective-permute-start.27 = (bf16[2,128,128]{2,1,0:T(8,128)(2,1)S(1)}, bf16[2,128,128]{2,1,0:T(8,128)(2,1)S(1)}, u32[]{:S(2)}, u32[]{:S(2)}) collective-permute-start(bf16[2,128,128]{2,1,0:T(8,128)(2,1)S(1)} %get-tuple-element.113), channel_id=1, source_target_pairs={{0,8},{8,16},{16,24},{24,0},{1,9},{9,17},{17,25},{25,1},{2,10},{10... | collective-permute-start | bytes 196616 | tf_op jit(solution)/shard_map/ppermute | solution.py:235
  132.6 16.8 %collective-permute-start.36 = (bf16[2,128,128]{2,1,0:T(8,128)(2,1)S(1)}, bf16[2,128,128]{2,1,0:T(8,128)(2,1)S(1)}, u32[]{:S(2)}, u32[]{:S(2)}) collective-permute-start(bf16[2,128,128]{2,1,0:T(8,128)(2,1)S(1)} %get-tuple-element.108), channel_id=1, source_target_pairs={{0,1},{1,2},{2,3},{3,4},{4,5},{5,6},{6,7},{7,0},{8,9},{9,10},{10,1... | collective-permute-start | bytes 196616 | tf_op jit(solution)/shard_map/ppermute | solution.py:234
  132.6 16.9 %collective-permute-start.37 = (bf16[2,128,128]{2,1,0:T(8,128)(2,1)S(1)}, bf16[2,128,128]{2,1,0:T(8,128)(2,1)S(1)}, u32[]{:S(2)}, u32[]{:S(2)}) collective-permute-start(bf16[2,128,128]{2,1,0:T(8,128)(2,1)S(1)} %get-tuple-element.107), channel_id=1, source_target_pairs={{0,8},{8,16},{16,24},{24,0},{1,9},{9,17},{17,25},{25,1},{2,10},{10... | collective-permute-start | bytes 196616 | tf_op jit(solution)/shard_map/ppermute | solution.py:235
  149.4 16.3 %collective-permute-start.28 = (bf16[2,128,128]{2,1,0:T(8,128)(2,1)S(1)}, bf16[2,128,128]{2,1,0:T(8,128)(2,1)S(1)}, u32[]{:S(2)}, u32[]{:S(2)}) collective-permute-start(bf16[2,128,128]{2,1,0:T(8,128)(2,1)S(1)} %get-tuple-element.112), channel_id=1, source_target_pairs={{0,1},{1,2},{2,3},{3,4},{4,5},{5,6},{6,7},{7,0},{8,9},{9,10},{10,1... | collective-permute-start | bytes 196616 | tf_op jit(solution)/shard_map/ppermute | solution.py:234
  149.5 18.5 %collective-permute-start.29 = (bf16[2,128,128]{2,1,0:T(8,128)(2,1)S(1)}, bf16[2,128,128]{2,1,0:T(8,128)(2,1)S(1)}, u32[]{:S(2)}, u32[]{:S(2)}) collective-permute-start(bf16[2,128,128]{2,1,0:T(8,128)(2,1)S(1)} %get-tuple-element.111), channel_id=1, source_target_pairs={{0,8},{8,16},{16,24},{24,0},{1,9},{9,17},{17,25},{25,1},{2,10},{10... | collective-permute-start | bytes 196616 | tf_op jit(solution)/shard_map/ppermute | solution.py:235
  165.7 18.9 %collective-permute-start.38 = (bf16[2,128,128]{2,1,0:T(8,128)(2,1)S(1)}, bf16[2,128,128]{2,1,0:T(8,128)(2,1)S(1)}, u32[]{:S(2)}, u32[]{:S(2)}) collective-permute-start(bf16[2,128,128]{2,1,0:T(8,128)(2,1)S(1)} %get-tuple-element.106), channel_id=1, source_target_pairs={{0,1},{1,2},{2,3},{3,4},{4,5},{5,6},{6,7},{7,0},{8,9},{9,10},{10,1... | collective-permute-start | bytes 196616 | tf_op jit(solution)/shard_map/ppermute | solution.py:234
  168.0 17.4 %collective-permute-start.39 = (bf16[2,128,128]{2,1,0:T(8,128)(2,1)S(1)}, bf16[2,128,128]{2,1,0:T(8,128)(2,1)S(1)}, u32[]{:S(2)}, u32[]{:S(2)}) collective-permute-start(bf16[2,128,128]{2,1,0:T(8,128)(2,1)S(1)} %get-tuple-element.105), channel_id=1, source_target_pairs={{0,8},{8,16},{16,24},{24,0},{1,9},{9,17},{17,25},{25,1},{2,10},{10... | collective-permute-start | bytes 196616 | tf_op jit(solution)/shard_map/ppermute | solution.py:235
  184.6 119.9 %collective-permute-start.30 = (bf16[1,256,128]{2,1,0:T(8,128)(2,1)}, bf16[1,256,128]{2,1,0:T(8,128)(2,1)}, u32[]{:S(2)}, u32[]{:S(2)}) collective-permute-start(bf16[1,256,128]{2,1,0:T(8,128)(2,1)} %get-tuple-element.110), channel_id=1, source_target_pairs={{0,2},{1,3},{2,4},{3,5},{4,6},{5,7},{6,0},{7,1},{8,10},{9,11},{10,... | collective-permute-start | bytes 196616 | tf_op jit(solution)/shard_map/ppermute | solution.py:325
  185.4 121.8 %collective-permute-start.32 = (bf16[1,256,128]{2,1,0:T(8,128)(2,1)}, bf16[1,256,128]{2,1,0:T(8,128)(2,1)}, u32[]{:S(2)}, u32[]{:S(2)}) collective-permute-start(bf16[1,256,128]{2,1,0:T(8,128)(2,1)} %get-tuple-element.109), channel_id=1, source_target_pairs={{0,3},{1,4},{2,5},{3,6},{4,7},{5,0},{6,1},{7,2},{8,11},{9,12},{10,... | collective-permute-start | bytes 196616 | tf_op jit(solution)/shard_map/ppermute | solution.py:325
  205.6 106.1 %collective-permute-start.40 = (bf16[1,256,128]{2,1,0:T(8,128)(2,1)}, bf16[1,256,128]{2,1,0:T(8,128)(2,1)}, u32[]{:S(2)}, u32[]{:S(2)}) collective-permute-start(bf16[1,256,128]{2,1,0:T(8,128)(2,1)} %get-tuple-element.104), channel_id=1, source_target_pairs={{0,4},{1,5},{2,6},{3,7},{4,0},{5,1},{6,2},{7,3},{8,12},{9,13},{10,... | collective-permute-start | bytes 196616 | tf_op jit(solution)/shard_map/ppermute | solution.py:325
  220.9 14.6 %collective-permute-start.20 = (bf16[2,128,128]{2,1,0:T(8,128)(2,1)S(1)}, bf16[2,128,128]{2,1,0:T(8,128)(2,1)S(1)}, u32[]{:S(2)}, u32[]{:S(2)}) collective-permute-start(bf16[2,128,128]{2,1,0:T(8,128)(2,1)S(1)} %get-tuple-element.118), channel_id=1, source_target_pairs={{0,1},{1,2},{2,3},{3,4},{4,5},{5,6},{6,7},{7,0},{8,9},{9,10},{10,1... | collective-permute-start | bytes 196616 | tf_op jit(solution)/shard_map/ppermute | solution.py:234
  221.0 18.4 %collective-permute-start.21 = (bf16[2,128,128]{2,1,0:T(8,128)(2,1)S(1)}, bf16[2,128,128]{2,1,0:T(8,128)(2,1)S(1)}, u32[]{:S(2)}, u32[]{:S(2)}) collective-permute-start(bf16[2,128,128]{2,1,0:T(8,128)(2,1)S(1)} %get-tuple-element.117), channel_id=1, source_target_pairs={{0,8},{8,16},{16,24},{24,0},{1,9},{9,17},{17,25},{25,1},{2,10},{10... | collective-permute-start | bytes 196616 | tf_op jit(solution)/shard_map/ppermute | solution.py:235
  235.5 20.2 %collective-permute-start.9 = (bf16[2,128,128]{2,1,0:T(8,128)(2,1)S(1)}, bf16[2,128,128]{2,1,0:T(8,128)(2,1)S(1)}, u32[]{:S(2)}, u32[]{:S(2)}) collective-permute-start(bf16[2,128,128]{2,1,0:T(8,128)(2,1)S(1)} %get-tuple-element.122), channel_id=1, source_target_pairs={{0,1},{1,2},{2,3},{3,4},{4,5},{5,6},{6,7},{7,0},{8,9},{9,10},{10,1... | collective-permute-start | bytes 196616 | tf_op jit(solution)/shard_map/ppermute | solution.py:234
  239.4 16.4 %collective-permute-start.10 = (bf16[2,128,128]{2,1,0:T(8,128)(2,1)S(1)}, bf16[2,128,128]{2,1,0:T(8,128)(2,1)S(1)}, u32[]{:S(2)}, u32[]{:S(2)}) collective-permute-start(bf16[2,128,128]{2,1,0:T(8,128)(2,1)S(1)} %get-tuple-element.121), channel_id=1, source_target_pairs={{0,8},{8,16},{16,24},{24,0},{1,9},{9,17},{17,25},{25,1},{2,10},{10... | collective-permute-start | bytes 196616 | tf_op jit(solution)/shard_map/ppermute | solution.py:235
  255.8 14.5 %collective-permute-start.22 = (bf16[2,128,128]{2,1,0:T(8,128)(2,1)S(1)}, bf16[2,128,128]{2,1,0:T(8,128)(2,1)S(1)}, u32[]{:S(2)}, u32[]{:S(2)}) collective-permute-start(bf16[2,128,128]{2,1,0:T(8,128)(2,1)S(1)} %get-tuple-element.116), channel_id=1, source_target_pairs={{0,1},{1,2},{2,3},{3,4},{4,5},{5,6},{6,7},{7,0},{8,9},{9,10},{10,1... | collective-permute-start | bytes 196616 | tf_op jit(solution)/shard_map/ppermute | solution.py:234
  255.8 16.3 %collective-permute-start.23 = (bf16[2,128,128]{2,1,0:T(8,128)(2,1)S(1)}, bf16[2,128,128]{2,1,0:T(8,128)(2,1)S(1)}, u32[]{:S(2)}, u32[]{:S(2)}) collective-permute-start(bf16[2,128,128]{2,1,0:T(8,128)(2,1)S(1)} %get-tuple-element.115), channel_id=1, source_target_pairs={{0,8},{8,16},{16,24},{24,0},{1,9},{9,17},{17,25},{25,1},{2,10},{10... | collective-permute-start | bytes 196616 | tf_op jit(solution)/shard_map/ppermute | solution.py:235
  270.3 17.8 %collective-permute-start.11 = (bf16[2,128,128]{2,1,0:T(8,128)(2,1)S(1)}, bf16[2,128,128]{2,1,0:T(8,128)(2,1)S(1)}, u32[]{:S(2)}, u32[]{:S(2)}) collective-permute-start(bf16[2,128,128]{2,1,0:T(8,128)(2,1)S(1)} %get-tuple-element.120), channel_id=1, source_target_pairs={{0,1},{1,2},{2,3},{3,4},{4,5},{5,6},{6,7},{7,0},{8,9},{9,10},{10,1... | collective-permute-start | bytes 196616 | tf_op jit(solution)/shard_map/ppermute | solution.py:234
  272.2 20.1 %collective-permute-start.12 = (bf16[2,128,128]{2,1,0:T(8,128)(2,1)S(1)}, bf16[2,128,128]{2,1,0:T(8,128)(2,1)S(1)}, u32[]{:S(2)}, u32[]{:S(2)}) collective-permute-start(bf16[2,128,128]{2,1,0:T(8,128)(2,1)S(1)} %get-tuple-element.119), channel_id=1, source_target_pairs={{0,8},{8,16},{16,24},{24,0},{1,9},{9,17},{17,25},{25,1},{2,10},{10... | collective-permute-start | bytes 196616 | tf_op jit(solution)/shard_map/ppermute | solution.py:235
  288.1 25.5 %collective-permute-start.42 = (bf16[1,256,128]{2,1,0:T(8,128)(2,1)S(1)}, bf16[1,256,128]{2,1,0:T(8,128)(2,1)S(1)}, u32[]{:S(2)}, u32[]{:S(2)}) collective-permute-start(bf16[1,256,128]{2,1,0:T(8,128)(2,1)S(1)} %copy-done.8), channel_id=1, source_target_pairs={{0,5},{1,6},{2,7},{3,0},{4,1},{5,2},{6,3},{7,4},{8,13},{9,14},{10,... | collective-permute-start | bytes 196616 | tf_op jit(solution)/shard_map/ppermute | solution.py:325
  292.3 22.0 %collective-permute-start.44 = (bf16[1,1536,128]{2,1,0:T(8,128)(2,1)S(1)}, bf16[1,1536,128]{2,1,0:T(8,128)(2,1)S(1)}, u32[]{:S(2)}, u32[]{:S(2)}) collective-permute-start(bf16[1,1536,128]{2,1,0:T(8,128)(2,1)S(1)} %get-tuple-element.80), channel_id=1, source_target_pairs={{0,2},{1,3},{2,4},{3,5},{4,6},{5,7},{6,0},{7,1},{8,10},{9,11},{10,... | collective-permute-start | bytes 1179656 | tf_op jit(solution)/shard_map/ppermute | solution.py:326
  304.5 31.7 %collective-permute-start.45 = (bf16[1,1536,128]{2,1,0:T(8,128)(2,1)S(1)}, bf16[1,1536,128]{2,1,0:T(8,128)(2,1)S(1)}, u32[]{:S(2)}, u32[]{:S(2)}) collective-permute-start(bf16[1,1536,128]{2,1,0:T(8,128)(2,1)S(1)} %get-tuple-element.79), channel_id=1, source_target_pairs={{0,3},{1,4},{2,5},{3,6},{4,7},{5,0},{6,1},{7,2},{8,11},{9,12},{10,... | collective-permute-start | bytes 1179656 | tf_op jit(solution)/shard_map/ppermute | solution.py:326
  307.1 36.8 %collective-permute-start.46 = (bf16[1,1536,128]{2,1,0:T(8,128)(2,1)S(1)}, bf16[1,1536,128]{2,1,0:T(8,128)(2,1)S(1)}, u32[]{:S(2)}, u32[]{:S(2)}) collective-permute-start(bf16[1,1536,128]{2,1,0:T(8,128)(2,1)S(1)} %get-tuple-element.78), channel_id=1, source_target_pairs={{0,4},{1,5},{2,6},{3,7},{4,0},{5,1},{6,2},{7,3},{8,12},{9,13},{10,... | collective-permute-start | bytes 1179656 | tf_op jit(solution)/shard_map/ppermute | solution.py:326
  311.7 40.2 %collective-permute-start.47 = (bf16[1,1536,128]{2,1,0:T(8,128)(2,1)S(1)}, bf16[1,1536,128]{2,1,0:T(8,128)(2,1)S(1)}, u32[]{:S(2)}, u32[]{:S(2)}) collective-permute-start(bf16[1,1536,128]{2,1,0:T(8,128)(2,1)S(1)} %get-tuple-element.77), channel_id=1, source_target_pairs={{0,5},{1,6},{2,7},{3,0},{4,1},{5,2},{6,3},{7,4},{8,13},{9,14},{10,... | collective-permute-start | bytes 1179656 | tf_op jit(solution)/shard_map/ppermute | solution.py:326
  (36 other events, 269.9 us)
